TPU v7x, 128 devices: a whole 4x4x4 slice. The times are simulated.
128 devices in a mesh: dp: 32 (over y, x, core), fsdp: 4 (over z).
Axes of the slice: x: 4, y: 4, z: 4, core: 2. Of those that a mesh axis runs over, the one named last changes fastest.
Arguments:
- memory: bfloat16 [16384, 4096], P('dp'), may hold values from -6 to 6
- key_weight: bfloat16 [4096, 2048], P('dp', 'fsdp'), may hold values from -0.09375 to 0.09375
- value_weight: bfloat16 [4096, 2048], P('dp', 'fsdp'), may hold values from -0.09375 to 0.09375
- query: bfloat16 [16384, 2048], P('dp', 'fsdp')
- grad_context: bfloat16 [16384, 2048], P('dp', 'fsdp')
- target_segment: int32 [32, 512], P('dp'), may hold values from 0 to 31, never falling along the last dimension, each value on 1 to 32 neighbouring positions
- memory_segment: int32 [32, 512], P('dp'), may hold values from 0 to 31, never falling along the last dimension, each value on 1 to 128 neighbouring positions
- example_pack: int32 [32, 32], replicated, may hold values from 0 to 31, as said below
- example_slot: int32 [32, 32], replicated, may hold values from 0 to 31, as said below
Outputs:
- context: bfloat16 [16384, 2048], P('dp', 'fsdp')
- grad_query: bfloat16 [16384, 2048], P('dp', 'fsdp')
- grad_key_weight: float32 [4096, 2048], P('dp', 'fsdp')
- grad_value_weight: float32 [4096, 2048], P('dp', 'fsdp')
- grad_memory: bfloat16 [16384, 4096], P(('dp', 'fsdp'))
Inputs may be any that keep to these rules, and one draw needn't show every extreme that they name: `target_segment`: rows of each target pack are ordered by example; every one of the 32 examples has 1 to 32 decoder rows, and some example has exactly 32. `memory_segment`: rows of each input pack are ordered by segment; every one of the 32 segments has 1 to 128 memory rows, and some segment has exactly 128. `example_pack`: the 32 examples of one target pack have their memory in 32 different input packs, and every input pack holds the memory of exactly 32 examples. `example_slot`: the examples whose memory lies in one input pack carry the segment numbers 0 to 31 of that pack, each once.
All inputs are finite; a program needn't handle non-finite values.
Results may differ from a plain program's by a relative error of at most 0.017.
Values may be sent and summed in bfloat16 or wider, within the bound.
No kernel may reach another device: no remote copies, remote signals or barrier semaphores. Data moves between devices by JAX's collectives and lax.ppermute only.
A program may use at most 128 MiB of HBM per device.

v0:
```python
import jax
import jax.numpy as jnp
from jax import lax
from jax.sharding import PartitionSpec as P

HD = 256
SCORE_SCALE = 0.0625
MASKED_SCORE = -1e30


def lookup(table, indices):
    positions = jnp.arange(table.shape[0], dtype=jnp.int32)
    return jnp.sum(jnp.where(indices[..., None] == positions, table, 0), axis=-1)


def slot_layout(segment, my_packs, peer_count, depth):
    example_ids = jnp.arange(my_packs.shape[0], dtype=jnp.int32)
    member = (segment[None, :] == example_ids[:, None]).astype(jnp.int32)
    counts = jnp.sum(member, axis=1)
    starts = jnp.cumsum(counts) - counts
    peer_ids = jnp.arange(peer_count, dtype=jnp.int32)
    matched = my_packs[None, :] == peer_ids[:, None]
    chosen = jnp.sum(jnp.where(matched, example_ids[None, :], 0), axis=1)
    present = jnp.any(matched, axis=1)
    offsets = jnp.arange(depth, dtype=jnp.int32)
    live = present[:, None] & (offsets[None, :] < lookup(counts, chosen)[:, None])
    source = jnp.where(live, lookup(starts, chosen)[:, None] + offsets[None, :], 0)
    positions = jnp.arange(segment.shape[0], dtype=jnp.int32)
    target_slot = lookup(my_packs, segment) * depth + positions - lookup(starts, segment)
    return (source, live, target_slot)


def to_slots(row_data, source, live):
    peer_count, depth = source.shape
    taken = jnp.take(row_data, source.reshape(-1), axis=0).reshape(
        peer_count, depth, row_data.shape[1]
    )
    return jnp.where(live[..., None], taken, jnp.zeros_like(taken))


def from_slots(slot_data, target_slot):
    flat_data = slot_data.reshape(-1, slot_data.shape[2])
    return jnp.take(flat_data, target_slot, axis=0)


def pair_scores(left, key_set):
    return jnp.einsum("trhd,khd->thrk", left, key_set, preferred_element_type=jnp.float32)


def apply_weights(weights, value_set):
    return jnp.einsum("thrk,khd->trhd", weights, value_set, preferred_element_type=jnp.float32)


def spread_back(weights, right):
    return jnp.einsum("thrk,trhd->khd", weights, right, preferred_element_type=jnp.float32)


def softmax_weights(query_set, key_set, valid):
    scores = pair_scores(query_set, key_set) * SCORE_SCALE
    scores = jnp.where(valid[:, None, None, :], scores, MASKED_SCORE)
    row_top = jnp.max(scores, axis=-1, keepdims=True)
    raised = jnp.exp(scores - row_top)
    return raised / jnp.sum(raised, axis=-1, keepdims=True)


def per_device(
    memory,
    key_weight,
    value_weight,
    query,
    grad_context,
    target_segment,
    memory_segment,
    example_pack,
    example_slot,
):
    peer_count = lax.axis_size("dp")
    my_index = lax.axis_index("dp")
    width = key_weight.shape[1]
    heads = width // HD
    row_count = memory.shape[0]
    depth = 2 * query.shape[0] // peer_count
    stacked = jnp.stack((key_weight, value_weight), axis=1)
    piece = lax.all_gather(stacked, "dp", axis=0, tiled=True)
    columns = memory
    projected = jnp.dot(
        columns, piece.reshape(piece.shape[0], 2 * width), preferred_element_type=jnp.float32
    )
    key_rows = projected[:, :width].astype(jnp.bfloat16).reshape(row_count, heads, HD)
    value_rows = projected[:, width:].astype(jnp.bfloat16).reshape(row_count, heads, HD)
    mem_segment = memory_segment[0]
    owned = example_pack == my_index
    wanted = jnp.where(
        jnp.any(owned, axis=1), jnp.sum(jnp.where(owned, example_slot, 0), axis=1), -1
    )
    valid = mem_segment[None, :] == wanted[:, None]
    my_packs = lax.dynamic_index_in_dim(example_pack, my_index, 0, keepdims=False)
    source, live, target_slot = slot_layout(target_segment[0], my_packs, peer_count, depth)
    outgoing = to_slots(query, source, live)
    piece = lax.all_to_all(outgoing, "dp", split_axis=0, concat_axis=0, tiled=True)
    query_set = piece.reshape(peer_count, piece.shape[1], heads, HD)
    weights = softmax_weights(query_set, key_rows, valid).astype(jnp.bfloat16)
    mixed = apply_weights(weights, value_rows)
    answers = mixed.astype(jnp.bfloat16).reshape(peer_count, piece.shape[1], width)
    arrived = piece
    returned = lax.all_to_all(answers, "dp", split_axis=0, concat_axis=0, tiled=True)
    context = from_slots(returned, target_slot)
    grad_outgoing = to_slots(grad_context, source, live)
    grad_arrived = lax.all_to_all(grad_outgoing, "dp", split_axis=0, concat_axis=0, tiled=True)
    query_set = arrived.reshape(peer_count, depth, heads, HD)
    grad_set = grad_arrived.reshape(peer_count, depth, heads, HD)
    probability = softmax_weights(query_set, key_rows, valid)
    rounded = probability.astype(jnp.bfloat16)
    grad_prob = pair_scores(grad_set, value_rows)
    row_delta = jnp.sum(probability * grad_prob, axis=-1, keepdims=True)
    grad_scores = (probability * (grad_prob - row_delta) * SCORE_SCALE).astype(jnp.bfloat16)
    slot_grad = (
        apply_weights(grad_scores, key_rows).astype(jnp.bfloat16).reshape(peer_count, depth, width)
    )
    grad_returned = lax.all_to_all(slot_grad, "dp", split_axis=0, concat_axis=0, tiled=True)
    grad_query = from_slots(grad_returned, target_slot)
    grad_keys = spread_back(grad_scores, query_set)
    grad_values = spread_back(rounded, grad_set)
    grad_kv = jnp.concatenate(
        [
            grad_keys.astype(jnp.bfloat16).reshape(row_count, width),
            grad_values.astype(jnp.bfloat16).reshape(row_count, width),
        ],
        axis=1,
    )
    columns = memory
    weight_grads = lax.psum_scatter(
        lax.dot_general(
            columns, grad_kv, (((0,), (0,)), ((), ())), preferred_element_type=jnp.float32
        ).astype(jnp.bfloat16),
        "dp",
        scatter_dimension=0,
        tiled=True,
    ).astype(jnp.float32)
    piece = lax.all_gather(stacked, "dp", axis=0, tiled=True)
    flat_piece = piece.reshape(piece.shape[0], 2 * width)
    partial_sums = lax.dot_general(
        grad_kv, flat_piece, (((1,), (1,)), ((), ())), preferred_element_type=jnp.float32
    )
    grad_memory = lax.psum_scatter(partial_sums, "fsdp", scatter_dimension=0, tiled=True)
    return (
        context,
        grad_query,
        weight_grads[:, :width],
        weight_grads[:, width:],
        grad_memory.astype(jnp.bfloat16),
    )


def solution(mesh):
    placed = (
        P("dp", None),
        P("dp", "fsdp"),
        P("dp", "fsdp"),
        P("dp", "fsdp"),
        P("dp", "fsdp"),
        P("dp", None),
        P("dp", None),
        P(),
        P(),
    )
    return jax.shard_map(
        per_device,
        mesh=mesh,
        in_specs=placed,
        out_specs=(
            P("dp", "fsdp"),
            P("dp", "fsdp"),
            P("dp", "fsdp"),
            P("dp", "fsdp"),
            P(("dp", "fsdp"), None),
        ),
        check_vma=False,
    )
```

profile of v0, /device:TPU:1, one launch (start us, length us, event | category | flops | bytes accessed | tf_op | source)
XLA Modules:
  0.0 347.4 jit_solution(4169301897632804495)
XLA Ops:
  7.2 0.0 copy-start
  7.2 0.0 all-gather.2.cloned.1.call-start
  7.2 1.1 copy.58
  8.3 1.0 copy.59
  9.3 0.7 pad_maximum_fusion.3
  10.1 0.0 all-gather.2.cloned.1.call-update
  10.1 0.8 convert_reduce_fusion
  10.9 0.1 copy.57
  11.0 0.1 reduce-window.9
  11.0 0.1 reduce
  11.2 0.7 dynamic-slice_bitcast_fusion
  11.9 0.1 fusion.33
  12.0 0.1 select_reduce_fusion.4
  12.1 0.2 select_reduce_fusion.3
  12.3 0.1 add_select_fusion
  12.4 0.1 select_n.74
  12.5 0.0 copy-start.2
  12.5 4.0 %gather_fusion.2 = bf16[1024,512]{1,0:T(8,128)(2,1)S(1)} fusion(bf16[512,512]{1,0:T(8,128)(2,1)S(1)} %copy-done, s32[1024]{0:T(1024)S(1)} %fusion.35), kind=kCustom, calls=%fused_computation.2.clone | custom fusion | bytes 2101248 | tf_op jit(solution)/shard_map/jit(_take)/gather | solution.py:35
  16.5 4.0 %gather_fusion = bf16[1024,512]{1,0:T(8,128)(2,1)S(1)} fusion(bf16[512,512]{1,0:T(8,128)(2,1)S(1)} %copy-done.2, s32[1024]{0:T(1024)S(1)} %fusion.35), kind=kCustom, calls=%fused_computation.clone | custom fusion | bytes 2101248 | tf_op jit(solution)/shard_map/jit(_take)/gather | solution.py:35
  20.4 0.1 fusion.34
  20.5 0.3 broadcast_select_fusion
  20.8 0.0 copy-start.6
  20.8 1.2 broadcast_select_fusion.2
  22.0 26.2 %all_to_all.20 = bf16[32,32,512]{2,1,0:T(8,128)(2,1)S(1)} all-to-all(bf16[32,32,512]{2,1,0:T(8,128)(2,1)S(1)} %get-tuple-element.40), channel_id=1, replica_groups=mesh['dp'=32,'fsdp'=4] {'dp'}, dimensions={0} | all-to-all | bytes 2097152 | tf_op jit(solution)/shard_map/all_to_all | solution.py:100
  48.3 4.4 %all-to-all-start.2 = ((bf16[32,32,512]{2,1,0:T(8,128)(2,1)}), bf16[32,32,512]{2,1,0:T(8,128)(2,1)S(1)}, u32[]{:S(2)}, u32[]{:S(2)}) async-start(bf16[32,32,512]{2,1,0:T(8,128)(2,1)} %get-tuple-element.39), calls=%async_computation.2 | async-start | bytes 2097152 | tf_op jit(solution)/shard_map/all_to_all | solution.py:109
  52.7 0.2 reduce-scatter.7.cloned.1.call-start
  53.0 0.1 select_reduce_fusion.5
  53.1 0.1 reduce_or.18
  53.2 0.1 broadcast_compare_fusion
  53.3 1.2 copy.93
  54.5 19.9 %all-to-all-done.2 = bf16[32,32,512]{2,1,0:T(8,128)(2,1)S(1)} async-done(((bf16[32,32,512]{2,1,0:T(8,128)(2,1)}), bf16[32,32,512]{2,1,0:T(8,128)(2,1)S(1)}, u32[]{:S(2)}, u32[]{:S(2)}) %all-to-all-start.2) | async-done | bytes 1048608 | tf_op jit(solution)/shard_map/all_to_all | solution.py:109
  74.4 1.1 copy.92
  75.5 17.4 %all-gather.2.cloned.1.call-done = bf16[4096,2,512]{0,2,1:T(8,128)(2,1)} async-done(((bf16[128,2,512]{0,2,1:T(8,128)(2,1)}), bf16[4096,2,512]{0,2,1:T(8,128)(2,1)}) %all-gather.2.cloned.1.call-update) | async-done | bytes 8388624 | tf_op jit(solution)/shard_map/all_gather | solution.py:84
  92.9 9.2 %fusion.19 = bf16[512,1024]{0,1:T(8,128)(2,1)S(1)} fusion(bf16[4096,1024]{0,1:T(8,128)(2,1)} %bitcast.94, bf16[512,4096]{1,0:T(8,128)(2,1)} %param.13), kind=kOutput, calls=%fused_computation.23 | convolution fusion | flops 4295491584 | bytes 13631488 | tf_op jit(solution)/shard_map/dot_general | solution.py:86
  102.1 0.1 fusion.44
  102.2 2.7 fusion.48
  104.8 0.7 fusion.47
  105.6 6.1 %fusion.46 = (f32[32,2,32]{2,0,1:T(8,128)S(1)}, f32[32,2,32,512]{3,2,0,1:T(8,128)S(1)}) fusion(f32[2,512,32,32]{1,3,2,0:T(8,128)S(1)} %bitcast.100, pred[32,512]{1,0:T(8,128)(4,1)S(1)} %broadcast_compare_fusion), kind=kOutput, calls=%fused_computation.77 | output fusion | flops 6291967 | bytes 8413184 | tf_op jit(solution)/shard_map/sub | solution.py:62
  111.6 2.2 fusion.26
  113.8 15.8 %fusion.27 = bf16[2,256,512]{2,1,0:T(8,128)(2,1)S(1)} fusion(f32[32,2,32,512]{3,2,0,1:T(8,128)} %bitcast.98, bf16[32,4,2,8,256]{4,3,2,1,0:T(8,128)(2,1)S(1)} %bitcast.102, f32[32,2,32,512]{3,2,0,1:T(8,128)} %copy-done.10, f32[32,2,32]{2,0,1:T(8,128)S(1)} %get-tuple-element.45), kind=kOutput, calls=%fused_computation.28 | convolution fusion | flops 544475648 | bytes 9969664 | tf_op jit(solution)/shard_map/thrk,trhd->khd/dot_general | solution.py:55
  129.7 9.6 %convert_bitcast_fusion = bf16[4096,1024]{0,1:T(8,128)(2,1)} fusion(bf16[512,4096]{1,0:T(8,128)(2,1)} %param.13, bf16[512,512]{0,1:T(8,128)(2,1)S(1)} %bitcast.112, bf16[512,512]{0,1:T(8,128)(2,1)S(1)} %bitcast.114), kind=kOutput, calls=%fused_computation.6 | convolution fusion | flops 4301258752 | bytes 13631488 | tf_op jit(solution)/shard_map/dot_general | solution.py:133
  139.3 11.9 %copy.82 = bf16[4096,1024]{1,0:T(8,128)(2,1)} copy(bf16[4096,1024]{0,1:T(8,128)(2,1)} %convert_bitcast_fusion) | data formatting | bytes 16777216
  151.2 0.0 reduce-scatter.7.cloned.1.call-update
  151.2 0.3 reduce-scatter.5.cloned.1.call-start
  151.5 10.2 %fusion.32 = f32[512,4096]{1,0:T(8,128)} fusion(bf16[4096,1024]{0,1:T(8,128)(2,1)} %bitcast.95, bf16[512,512]{0,1:T(8,128)(2,1)S(1)} %bitcast.113, bf16[512,512]{0,1:T(8,128)(2,1)S(1)} %bitcast.115), kind=kOutput, calls=%fused_computation.38 | convolution fusion | flops 4297064448 | bytes 17825792 | tf_op jit(solution)/shard_map/dot_general | solution.py:142
  161.7 0.0 reduce-scatter.5.cloned.1.call-update
  161.7 17.8 %fusion.20 = bf16[2,32,4,8,256]{4,3,2,1,0:T(8,128)(2,1)S(1)} fusion(bf16[512,2,256,1]{0,2,3,1:T(8,128)(2,1)S(1)} %bitcast.111, f32[32,2,32,512]{3,2,0,1:T(8,128)} %bitcast.99, f32[32,2,32,512]{3,2,0,1:T(8,128)} %copy-done.10, f32[32,2,32]{2,0,1:T(8,128)S(1)} %get-tuple-element.45), kind=kOutput, calls=%fused_computation.24 | convolution fusion | flops 544737792 | bytes 9969664 | tf_op jit(solution)/shard_map/thrk,khd->trhd/dot_general | solution.py:51
  179.5 1.1 copy.87
  180.6 5.5 %all-to-all-start.3 = ((bf16[32,32,512]{2,1,0:T(8,128)(2,1)}), bf16[32,32,512]{2,1,0:T(8,128)(2,1)S(1)}, u32[]{:S(2)}, u32[]{:S(2)}) async-start(bf16[32,32,512]{2,1,0:T(8,128)(2,1)} %bitcast.54), calls=%async_computation.3 | async-start | bytes 2097152 | tf_op jit(solution)/shard_map/all_to_all | solution.py:120
  186.1 3.2 fusion.18
  189.3 1.1 copy.86
  190.3 12.9 %all-to-all-done.3 = bf16[32,32,512]{2,1,0:T(8,128)(2,1)S(1)} async-done(((bf16[32,32,512]{2,1,0:T(8,128)(2,1)}), bf16[32,32,512]{2,1,0:T(8,128)(2,1)S(1)}, u32[]{:S(2)}, u32[]{:S(2)}) %all-to-all-start.3) | async-done | bytes 1048608 | tf_op jit(solution)/shard_map/all_to_all | solution.py:120
  203.3 4.0 %all-to-all-start.1 = ((bf16[32,32,512]{2,1,0:T(8,128)(2,1)}), bf16[32,32,512]{2,1,0:T(8,128)(2,1)S(1)}, u32[]{:S(2)}, u32[]{:S(2)}) async-start(bf16[32,32,512]{2,1,0:T(8,128)(2,1)} %bitcast.105), calls=%async_computation.1 | async-start | bytes 2097152 | tf_op jit(solution)/shard_map/all_to_all | solution.py:106
  207.3 0.1 select_reduce_fusion.1
  207.4 2.0 gather_fusion.3
  209.4 23.8 %all-to-all-done.1 = bf16[32,32,512]{2,1,0:T(8,128)(2,1)S(1)} async-done(((bf16[32,32,512]{2,1,0:T(8,128)(2,1)}), bf16[32,32,512]{2,1,0:T(8,128)(2,1)S(1)}, u32[]{:S(2)}, u32[]{:S(2)}) %all-to-all-start.1) | async-done | bytes 1048608 | tf_op jit(solution)/shard_map/all_to_all | solution.py:106
  233.1 2.0 gather_fusion.1
  235.1 1.1 broadcast_select_fusion.4
  236.2 17.4 %reduce-scatter.7.cloned.1.call-done = bf16[128,1024]{1,0:T(8,128)(2,1)} async-done(((bf16[4096,1024]{1,0:T(8,128)(2,1)}), bf16[128,1024]{1,0:T(8,128)(2,1)}) %reduce-scatter.7.cloned.1.call-update) | async-done | bytes 262160
  253.7 1.1 copy.83
  254.8 0.8 copy.71
  255.7 0.8 copy.70
  256.5 81.6 %reduce-scatter.5.cloned.1.call-done = f32[128,4096]{1,0:T(8,128)} async-done(((f32[512,4096]{1,0:T(8,128)}), f32[128,4096]{1,0:T(8,128)}) %reduce-scatter.5.cloned.1.call-update) | async-done | bytes 2097168 | tf_op jit(solution)/shard_map/reduce_scatter | solution.py:145
  338.2 2.7 convert_element_type.62
  (26 shorter events, 0.1 us)
Async XLA Ops:
  7.2 5.3 %copy-start = (bf16[512,512]{1,0:T(8,128)(2,1)S(1)}, bf16[512,512]{1,0:T(8,128)(2,1)}, u32[]{:S(2)}) copy-start(bf16[512,512]{1,0:T(8,128)(2,1)} %param.17) | copy-start | bytes 1572868
  7.2 85.7 %all-gather.2.cloned.1.call-start = ((), (), s32[]{:S(2)}) async-start(), calls=%async_computation.6 | async-start | bytes 8650752 | tf_op jit(solution)/shard_map/all_gather | solution.py:84
  12.5 4.0 %copy-start.2 = (bf16[512,512]{1,0:T(8,128)(2,1)S(1)}, bf16[512,512]{1,0:T(8,128)(2,1)}, u32[]{:S(2)}) copy-start(bf16[512,512]{1,0:T(8,128)(2,1)} %param.16) | copy-start | bytes 1572868
  20.8 32.1 %copy-start.6 = (s32[32,32]{1,0:T(8,128)S(1)}, s32[32,32]{1,0:T(8,128)}, u32[]{:S(2)}) copy-start(s32[32,32]{1,0:T(8,128)} %param.20) | copy-start | bytes 12292
  20.8 32.1 %copy-start.7 = (s32[32,32]{1,0:T(8,128)S(1)}, s32[32,32]{1,0:T(8,128)}, u32[]{:S(2)}) copy-start(s32[32,32]{1,0:T(8,128)} %param.21) | copy-start | bytes 12292
  20.8 32.4 %copy-start.9 = (s32[1,512]{1,0:T(1,128)S(1)}, s32[1,512]{1,0:T(1,128)}, u32[]{:S(2)}) copy-start(s32[1,512]{1,0:T(1,128)} %param.19) | copy-start | bytes 6148
  48.3 26.1 %all-to-all-start.2 = ((bf16[32,32,512]{2,1,0:T(8,128)(2,1)}), bf16[32,32,512]{2,1,0:T(8,128)(2,1)S(1)}, u32[]{:S(2)}, u32[]{:S(2)}) async-start(bf16[32,32,512]{2,1,0:T(8,128)(2,1)} %get-tuple-element.39), calls=%async_computation.2 | async-start | bytes 2097152 | tf_op jit(solution)/shard_map/all_to_all | solution.py:109
  52.7 200.9 %reduce-scatter.7.cloned.1.call-start = ((), (), s32[]{:S(2)}) async-start(), calls=%async_computation.8 | async-start | bytes 8650752
  92.9 9.3 %copy-start.4 = (bf16[32,4,2,8,256]{4,3,1,0,2:T(8,128)(2,1)S(1)}, bf16[32,4,2,8,256]{4,3,1,0,2:T(8,128)(2,1)}, u32[]{:S(2)}) copy-start(bf16[32,4,2,8,256]{4,3,1,0,2:T(8,128)(2,1)} %copy.92) | copy-start | bytes 3145732
  102.1 2.8 copy-start.3
  111.6 2.2 copy-start.10
  113.8 15.8 %copy-start.5 = (bf16[2,256,512]{2,1,0:T(8,128)(2,1)S(1)}, bf16[2,256,512]{2,1,0:T(8,128)(2,1)}, u32[]{:S(2)}) copy-start(bf16[2,256,512]{2,1,0:T(8,128)(2,1)} %fusion.26) | copy-start | bytes 1572868
  151.2 186.9 %reduce-scatter.5.cloned.1.call-start = ((), (), s32[]{:S(2)}) async-start(), calls=%async_computation.7 | async-start | bytes 10485760 | tf_op jit(solution)/shard_map/reduce_scatter | solution.py:145
  180.6 22.7 %all-to-all-start.3 = ((bf16[32,32,512]{2,1,0:T(8,128)(2,1)}), bf16[32,32,512]{2,1,0:T(8,128)(2,1)S(1)}, u32[]{:S(2)}, u32[]{:S(2)}) async-start(bf16[32,32,512]{2,1,0:T(8,128)(2,1)} %bitcast.54), calls=%async_computation.3 | async-start | bytes 2097152 | tf_op jit(solution)/shard_map/all_to_all | solution.py:120
  189.3 18.0 %copy-start.8 = (s32[1,512]{1,0:T(1,128)S(1)}, s32[1,512]{1,0:T(1,128)}, u32[]{:S(2)}) copy-start(s32[1,512]{1,0:T(1,128)} %param.18) | copy-start | bytes 6148
  203.3 29.9 %all-to-all-start.1 = ((bf16[32,32,512]{2,1,0:T(8,128)(2,1)}), bf16[32,32,512]{2,1,0:T(8,128)(2,1)S(1)}, u32[]{:S(2)}, u32[]{:S(2)}) async-start(bf16[32,32,512]{2,1,0:T(8,128)(2,1)} %bitcast.105), calls=%async_computation.1 | async-start | bytes 2097152 | tf_op jit(solution)/shard_map/all_to_all | solution.py:106
  233.1 107.7 %copy-start.1 = (bf16[512,512]{1,0:T(8,128)(2,1)S(1)}, bf16[512,512]{1,0:T(8,128)(2,1)}, u32[]{:S(2)}) copy-start(bf16[512,512]{1,0:T(8,128)(2,1)} %param.17) | copy-start | bytes 1572868
Sparse Core Ops, SparseCore 0:
  10.8 82.0 all-gather.1
  151.4 102.2 reduce-scatter.6
  256.3 81.8 reduce-scatter.4
where the time goes:
time: 348 us; the launch traced here: 347 us
  waiting for transfers between devices  173 us (50%)
  matrix products  71.3 us (20%)
  local copies, waits for them, and re-layouts  34.2 us (10%)
  blocking collectives  26.2 us (8%)
  starting transfers between devices  14.4 us (4%)
  other arithmetic  14.1 us (4%)
  between operations  14.1 us (4%)
    reduce_scatter x1, waiting for transfers between devices, per_device(): lax.psum_scatter(partial_sums, 'fsdp', scatter_dimension=0, tiled=True)  81.6 us
    all_to_all x1, blocking collectives, per_device(): lax.all_to_all(outgoing, 'dp', split_axis=0, concat_axis=0, tiled=True)  26.2 us
    all_to_all x1, waiting for transfers between devices, per_device(): lax.all_to_all(answers, 'dp', split_axis=0, concat_axis=0, tiled=True)  23.8 us
    dot_general x2, matrix products, apply_weights(): jnp.einsum('thrk,khd->trhd', weights, value_set, preferred_element_type=j...  21 us
    all_to_all x1, waiting for transfers between devices, per_device(): lax.all_to_all(grad_outgoing, 'dp', split_axis=0, concat_axis=0, tiled=True)  19.9 us
    dot_general x2, matrix products, spread_back(): jnp.einsum('thrk,trhd->khd', weights, right, preferred_element_type=jnp.f...  18 us
    unnamed x4, waiting for transfers between devices  17.5 us
    all_gather x1, waiting for transfers between devices, per_device(): piece = lax.all_gather(stacked, 'dp', axis=0, tiled=True)  17.4 us
  transfers between devices with their start and end apart: 6, of which 6 were waited for; matrix products, arithmetic and copies ran while one was open for 16% of the time, Pallas kernels for 0%

commit v1 on v0

--- a/solution.py
+++ b/solution.py
@@ -81,7 +81,9 @@
     row_count = memory.shape[0]
     depth = 2 * query.shape[0] // peer_count
     stacked = jnp.stack((key_weight, value_weight), axis=1)
-    piece = lax.all_gather(stacked, "dp", axis=0, tiled=True)
+    piece = jnp.concatenate(
+        lax.all_to_all(jnp.stack([stacked] * lax.axis_size("dp")), "dp", 0, 0), axis=0
+    )
     columns = memory
     projected = jnp.dot(
         columns, piece.reshape(piece.shape[0], 2 * width), preferred_element_type=jnp.float32

time: 348 us -> 454 us (1.30)
  waiting for transfers between devices: 173 us -> 253 us
  local copies, waits for them, and re-layouts: 34.2 us -> 52.6 us
  starting transfers between devices: 14.4 us -> 25.2 us
    all_to_all x1 -> x2, waiting for transfers between devices: 19.9 us -> 118 us  [the longest x1 96.9 us: per_device(): lax.all_to_all(jnp.stack([stacked] * lax.axis_size('dp')), 'dp', 0, 0)]
    all_gather x1, waiting for transfers between devices: 17.4 us -> 0.02 us  [per_device(): piece = lax.all_gather(stacked, 'dp', axis=0, tiled=True)]
    unnamed x28 -> x31, local copies, waits for them, and re-layouts: 16.9 us -> 26.6 us
    another operation x1 -> x3, local copies, waits for them, and re-layouts: 0.09 us -> 8.84 us  [the longest x1 8.56 us: per_device(): jnp.stack([stacked] * lax.axis_size('dp'))]
    all_to_all x1 -> x2, starting transfers between devices: 4.43 us -> 10.7 us  [the longest x1 6.28 us: per_device(): lax.all_to_all(jnp.stack([stacked] * lax.axis_size('dp')), 'dp', 0, 0)]
    all_to_all x1, starting transfers between devices: 5.51 us -> 10.3 us  [per_device(): lax.all_to_all(slot_grad, 'dp', split_axis=0, concat_axis=0, tiled=True)]
  transfers between devices with their start and end apart: 6 -> 7, of which waited for: 6 -> 6; matrix products, arithmetic and copies ran while one was open for 16% -> 28% of each run, Pallas kernels for 0% -> 0%
where the time goes in v1:
time: 454 us; the launch traced here: 452 us
  waiting for transfers between devices  253 us (56%)
  matrix products  70 us (15%)
  local copies, waits for them, and re-layouts  52.6 us (12%)
  blocking collectives  26.2 us (6%)
  starting transfers between devices  25.2 us (6%)
  between operations  14.1 us (3%)
  other arithmetic  11.3 us (2%)
    all_to_all x1, waiting for transfers between devices, per_device(): lax.all_to_all(jnp.stack([stacked] * lax.axis_size('dp')), 'dp', 0, 0)  96.9 us
    reduce_scatter x1, waiting for transfers between devices, per_device(): lax.psum_scatter(partial_sums, 'fsdp', scatter_dimension=0, tiled=True)  81.7 us
    unnamed x31, local copies, waits for them, and re-layouts  26.6 us
    all_to_all x1, blocking collectives, per_device(): lax.all_to_all(grad_outgoing, 'dp', split_axis=0, concat_axis=0, tiled=True)  26.2 us
    all_to_all x1, waiting for transfers between devices, per_device(): lax.all_to_all(answers, 'dp', split_axis=0, concat_axis=0, tiled=True)  22.8 us
    all_to_all x1, waiting for transfers between devices, per_device(): lax.all_to_all(outgoing, 'dp', split_axis=0, concat_axis=0, tiled=True)  21.5 us
    dot_general x2, matrix products, apply_weights(): jnp.einsum('thrk,khd->trhd', weights, value_set, preferred_element_type=j...  20.8 us
    dot_general x2, matrix products, spread_back(): jnp.einsum('thrk,trhd->khd', weights, right, preferred_element_type=jnp.f...  19.7 us
  transfers between devices with their start and end apart: 7, of which 6 were waited for; matrix products, arithmetic and copies ran while one was open for 28% of the time, Pallas kernels for 0%

profile of v1, /device:TPU:1, one launch (start us, length us, event | category | flops | bytes accessed | tf_op | source)
XLA Modules:
  0.0 452.5 jit_solution(2617094448407533233)
XLA Ops:
  7.2 0.0 all-gather.2.cloned.1.call-start
  7.2 1.1 copy.62
  8.3 1.0 copy.61
  9.3 0.7 pad_maximum_fusion.3
  10.1 0.7 dynamic-slice_bitcast_fusion
  10.8 0.1 select_reduce_fusion.4
  10.9 0.1 fusion.33
  11.0 0.8 convert_reduce_fusion
  11.8 0.1 copy.60
  11.9 0.1 reduce-window.9
  12.0 0.1 reduce
  12.1 0.2 select_reduce_fusion.3
  12.3 0.1 add_select_fusion
  12.4 0.1 select_n.74
  12.5 0.1 fusion.34
  12.6 4.0 gather_fusion.2
  16.6 4.0 gather_fusion
  20.5 0.3 broadcast_select_fusion
  20.8 1.2 broadcast_select_fusion.2
  22.0 26.2 %all_to_all.25 = bf16[32,32,512]{2,1,0:T(8,128)(2,1)S(1)} all-to-all(bf16[32,32,512]{2,1,0:T(8,128)(2,1)S(1)} %get-tuple-element.39), channel_id=1, replica_groups=mesh['dp'=32,'fsdp'=4] {'dp'}, dimensions={0} | all-to-all | bytes 2097152 | tf_op jit(solution)/shard_map/all_to_all | solution.py:111
  48.3 4.4 all-to-all-start.1
  52.7 0.2 copy.63
  52.9 21.5 %all-to-all-done.1 = bf16[32,32,512]{2,1,0:T(8,128)(2,1)S(1)} async-done(((bf16[32,32,512]{2,1,0:T(8,128)(2,1)}), bf16[32,32,512]{2,1,0:T(8,128)(2,1)S(1)}, u32[]{:S(2)}, u32[]{:S(2)}) %all-to-all-start.1) | async-done | bytes 1048608 | tf_op jit(solution)/shard_map/all_to_all | solution.py:102
  74.4 8.6 %stack.11 = bf16[32,128,2,512]{3,2,1,0:T(2,128)(2,1)} broadcast(bf16[128,2,512]{2,1,0:T(2,128)(2,1)S(1)} %copy.63), dimensions={1,2,3} | broadcast | bytes 8650752 | tf_op jit(solution)/shard_map/stack | solution.py:85
  82.9 6.3 %all-to-all-start = ((bf16[32,128,2,512]{3,2,1,0:T(2,128)(2,1)}), bf16[32,128,2,512]{3,2,1,0:T(2,128)(2,1)}, u32[]{:S(2)}, u32[]{:S(2)}) async-start(bf16[32,128,2,512]{3,2,1,0:T(2,128)(2,1)} %stack.11), calls=%async_computation | async-start | bytes 16777216 | tf_op jit(solution)/shard_map/all_to_all | solution.py:85
  89.2 0.2 reduce-scatter.7.cloned.1.call-start
  89.5 0.1 select_reduce_fusion.5
  89.6 0.1 reduce_or.18
  89.7 0.1 broadcast_compare_fusion
  89.8 1.1 copy.97
  90.9 1.2 copy.98
  92.1 96.9 %all-to-all-done = bf16[32,128,2,512]{3,2,1,0:T(2,128)(2,1)} async-done(((bf16[32,128,2,512]{3,2,1,0:T(2,128)(2,1)}), bf16[32,128,2,512]{3,2,1,0:T(2,128)(2,1)}, u32[]{:S(2)}, u32[]{:S(2)}) %all-to-all-start) | async-done | bytes 8388640 | tf_op jit(solution)/shard_map/all_to_all | solution.py:85
  189.0 9.3 %copy.92 = bf16[512,8,2,512]{3,1,2,0:T(8,128)(2,1)} copy(bf16[512,8,2,512]{3,2,1,0:T(2,128)(2,1)} %bitcast.56) | data formatting | bytes 16777216
  198.3 9.2 %fusion.19 = bf16[512,1024]{0,1:T(8,128)(2,1)S(1)} fusion(bf16[4096,1024]{1,0:T(8,128)(2,1)} %bitcast.98, bf16[512,4096]{1,0:T(8,128)(2,1)} %param.13), kind=kOutput, calls=%fused_computation.23 | convolution fusion | flops 4295491584 | bytes 13631488 | tf_op jit(solution)/shard_map/dot_general | solution.py:88
  207.5 0.1 fusion.44
  207.6 2.7 fusion.48
  210.3 0.7 fusion.47
  211.0 3.3 fusion.46
  214.3 16.5 %fusion.27 = bf16[2,256,512]{2,1,0:T(8,128)(2,1)} fusion(f32[32,2,32,512]{3,2,0,1:T(8,128)} %bitcast.101, bf16[32,4,2,8,256]{4,3,2,1,0:T(8,128)(2,1)S(1)} %bitcast.107, f32[32,2,32,512]{3,2,0,1:T(8,128)} %get-tuple-element.46, f32[32,2,32]{2,0,1:T(8,128)S(1)} %get-tuple-element.45), kind=kOutput, calls=%fused_computation.28 | convolution fusion | flops 544475648 | bytes 9969664 | tf_op jit(solution)/shard_map/thrk,trhd->khd/dot_general | solution.py:55
  230.9 3.2 fusion.26
  234.1 0.4 copy-done.11
  234.5 6.7 %convert_bitcast_fusion = bf16[4096,1024]{0,1:T(8,128)(2,1)} fusion(bf16[512,4096]{1,0:T(8,128)(2,1)S(1)} %copy-done.11, bf16[512,512]{0,1:T(8,128)(2,1)S(1)} %bitcast.117, bf16[512,512]{0,1:T(8,128)(2,1)S(1)} %bitcast.115), kind=kOutput, calls=%fused_computation.6 | convolution fusion | flops 4301258752 | bytes 13631488 | tf_op jit(solution)/shard_map/dot_general | solution.py:135
  241.2 11.9 %copy.86 = bf16[4096,1024]{1,0:T(8,128)(2,1)} copy(bf16[4096,1024]{0,1:T(8,128)(2,1)} %convert_bitcast_fusion) | data formatting | bytes 16777216
  253.1 0.0 reduce-scatter.5.cloned.1.call-start
  253.2 0.0 all-gather.2.cloned.1.call-done
  253.2 10.2 %fusion.32 = f32[512,4096]{1,0:T(8,128)} fusion(bf16[4096,1024]{0,1:T(8,128)(2,1)} %bitcast.97, bf16[512,512]{0,1:T(8,128)(2,1)S(1)} %bitcast.118, bf16[512,512]{0,1:T(8,128)(2,1)S(1)} %bitcast.116), kind=kOutput, calls=%fused_computation.38 | convolution fusion | flops 4297064448 | bytes 17825792 | tf_op jit(solution)/shard_map/dot_general | solution.py:144
  263.4 17.6 %fusion.20 = bf16[2,32,4,8,256]{4,3,2,1,0:T(8,128)(2,1)S(1)} fusion(bf16[512,2,256,1]{0,2,3,1:T(8,128)(2,1)S(1)} %bitcast.114, f32[32,2,32,512]{3,2,0,1:T(8,128)} %bitcast.102, f32[32,2,32,512]{3,2,0,1:T(8,128)} %get-tuple-element.46, f32[32,2,32]{2,0,1:T(8,128)S(1)} %get-tuple-element.45), kind=kOutput, calls=%fused_computation.24 | convolution fusion | flops 544737792 | bytes 9969664 | tf_op jit(solution)/shard_map/thrk,khd->trhd/dot_general | solution.py:51
  281.0 1.1 copy.91
  282.1 10.3 %all-to-all-start.4 = ((bf16[32,32,512]{2,1,0:T(8,128)(2,1)}), bf16[32,32,512]{2,1,0:T(8,128)(2,1)S(1)}, u32[]{:S(2)}, u32[]{:S(2)}) async-start(bf16[32,32,512]{2,1,0:T(8,128)(2,1)} %bitcast.54), calls=%async_computation.4 | async-start | bytes 2097152 | tf_op jit(solution)/shard_map/all_to_all | solution.py:122
  292.3 3.2 fusion.18
  295.5 1.1 copy.90
  296.6 13.0 %all-to-all-done.4 = bf16[32,32,512]{2,1,0:T(8,128)(2,1)S(1)} async-done(((bf16[32,32,512]{2,1,0:T(8,128)(2,1)}), bf16[32,32,512]{2,1,0:T(8,128)(2,1)S(1)}, u32[]{:S(2)}, u32[]{:S(2)}) %all-to-all-start.4) | async-done | bytes 1048608 | tf_op jit(solution)/shard_map/all_to_all | solution.py:122
  309.6 4.0 all-to-all-start.2
  313.6 0.1 select_reduce_fusion.1
  313.7 2.0 gather_fusion.3
  315.7 22.8 %all-to-all-done.2 = bf16[32,32,512]{2,1,0:T(8,128)(2,1)S(1)} async-done(((bf16[32,32,512]{2,1,0:T(8,128)(2,1)}), bf16[32,32,512]{2,1,0:T(8,128)(2,1)S(1)}, u32[]{:S(2)}, u32[]{:S(2)}) %all-to-all-start.2) | async-done | bytes 1048608 | tf_op jit(solution)/shard_map/all_to_all | solution.py:108
  338.5 2.0 gather_fusion.1
  340.5 1.1 broadcast_select_fusion.4
  341.6 17.1 %reduce-scatter.7.cloned.1.call-done = bf16[128,1024]{1,0:T(8,128)(2,1)} async-done(((bf16[4096,1024]{1,0:T(8,128)(2,1)}), bf16[128,1024]{1,0:T(8,128)(2,1)}) %reduce-scatter.7.cloned.1.call-update) | async-done | bytes 262160
  358.7 1.1 copy.87
  359.9 0.8 copy.74
  360.7 0.8 copy.75
  361.6 81.7 %reduce-scatter.5.cloned.1.call-done = f32[128,4096]{1,0:T(8,128)} async-done(((f32[512,4096]{1,0:T(8,128)}), f32[128,4096]{1,0:T(8,128)}) %reduce-scatter.5.cloned.1.call-update) | async-done | bytes 2097168 | tf_op jit(solution)/shard_map/reduce_scatter | solution.py:147
  443.2 2.7 convert_element_type.62
  (33 shorter events, 0.2 us)
Async XLA Ops:
  7.2 5.4 %copy-start = (bf16[512,512]{1,0:T(8,128)(2,1)S(1)}, bf16[512,512]{1,0:T(8,128)(2,1)}, u32[]{:S(2)}) copy-start(bf16[512,512]{1,0:T(8,128)(2,1)} %param.17) | copy-start | bytes 1572868
  7.2 246.0 %all-gather.2.cloned.1.call-start = ((), (), s32[]{:S(2)}) async-start(), calls=%async_computation.7 | async-start | bytes 8650752 | tf_op jit(solution)/shard_map/all_gather | solution.py:142
  12.6 4.0 copy-start.2
  20.8 31.9 %copy-start.5 = (bf16[128,2,512]{0,2,1:T(8,128)(2,1)S(1)}, bf16[128,2,512]{0,2,1:T(8,128)(2,1)}, u32[]{:S(2)}) copy-start(bf16[128,2,512]{0,2,1:T(8,128)(2,1)} %pad_maximum_fusion.3) | copy-start | bytes 786436
  48.3 26.1 %all-to-all-start.1 = ((bf16[32,32,512]{2,1,0:T(8,128)(2,1)}), bf16[32,32,512]{2,1,0:T(8,128)(2,1)S(1)}, u32[]{:S(2)}, u32[]{:S(2)}) async-start(bf16[32,32,512]{2,1,0:T(8,128)(2,1)} %get-tuple-element.40), calls=%async_computation.1 | async-start | bytes 2097152 | tf_op jit(solution)/shard_map/all_to_all | solution.py:102
  82.9 6.5 %copy-start.7 = (s32[32,32]{1,0:T(8,128)S(1)}, s32[32,32]{1,0:T(8,128)}, u32[]{:S(2)}) copy-start(s32[32,32]{1,0:T(8,128)} %param.20) | copy-start | bytes 12292
  82.9 6.5 %copy-start.8 = (s32[32,32]{1,0:T(8,128)S(1)}, s32[32,32]{1,0:T(8,128)}, u32[]{:S(2)}) copy-start(s32[32,32]{1,0:T(8,128)} %param.21) | copy-start | bytes 12292
  82.9 6.8 %copy-start.10 = (s32[1,512]{1,0:T(1,128)S(1)}, s32[1,512]{1,0:T(1,128)}, u32[]{:S(2)}) copy-start(s32[1,512]{1,0:T(1,128)} %param.19) | copy-start | bytes 6148
  82.9 106.1 %all-to-all-start = ((bf16[32,128,2,512]{3,2,1,0:T(2,128)(2,1)}), bf16[32,128,2,512]{3,2,1,0:T(2,128)(2,1)}, u32[]{:S(2)}, u32[]{:S(2)}) async-start(bf16[32,128,2,512]{3,2,1,0:T(2,128)(2,1)} %stack.11), calls=%async_computation | async-start | bytes 16777216 | tf_op jit(solution)/shard_map/all_to_all | solution.py:85
  89.2 269.5 %reduce-scatter.7.cloned.1.call-start = ((), (), s32[]{:S(2)}) async-start(), calls=%async_computation.9 | async-start | bytes 8650752
  198.3 9.3 %copy-start.4 = (bf16[32,4,2,8,256]{4,3,1,0,2:T(8,128)(2,1)S(1)}, bf16[32,4,2,8,256]{4,3,1,0,2:T(8,128)(2,1)}, u32[]{:S(2)}) copy-start(bf16[32,4,2,8,256]{4,3,1,0,2:T(8,128)(2,1)} %copy.97) | copy-start | bytes 3145732
  207.5 2.8 copy-start.3
  230.8 3.2 copy-start.6
  230.8 3.6 copy-start.11
  253.1 190.1 %reduce-scatter.5.cloned.1.call-start = ((), (), s32[]{:S(2)}) async-start(), calls=%async_computation.8 | async-start | bytes 10485760 | tf_op jit(solution)/shard_map/reduce_scatter | solution.py:147
  282.1 27.5 %all-to-all-start.4 = ((bf16[32,32,512]{2,1,0:T(8,128)(2,1)}), bf16[32,32,512]{2,1,0:T(8,128)(2,1)S(1)}, u32[]{:S(2)}, u32[]{:S(2)}) async-start(bf16[32,32,512]{2,1,0:T(8,128)(2,1)} %bitcast.54), calls=%async_computation.4 | async-start | bytes 2097152 | tf_op jit(solution)/shard_map/all_to_all | solution.py:122
  295.5 18.1 %copy-start.9 = (s32[1,512]{1,0:T(1,128)S(1)}, s32[1,512]{1,0:T(1,128)}, u32[]{:S(2)}) copy-start(s32[1,512]{1,0:T(1,128)} %param.18) | copy-start | bytes 6148
  309.6 28.9 %all-to-all-start.2 = ((bf16[32,32,512]{2,1,0:T(8,128)(2,1)}), bf16[32,32,512]{2,1,0:T(8,128)(2,1)S(1)}, u32[]{:S(2)}, u32[]{:S(2)}) async-start(bf16[32,32,512]{2,1,0:T(8,128)(2,1)} %bitcast.108), calls=%async_computation.2 | async-start | bytes 2097152 | tf_op jit(solution)/shard_map/all_to_all | solution.py:108
  338.5 107.4 %copy-start.1 = (bf16[512,512]{1,0:T(8,128)(2,1)S(1)}, bf16[512,512]{1,0:T(8,128)(2,1)}, u32[]{:S(2)}) copy-start(bf16[512,512]{1,0:T(8,128)(2,1)} %param.17) | copy-start | bytes 1572868
Sparse Core Ops, SparseCore 0:
  10.8 82.0 all-gather.1
  253.2 105.4 reduce-scatter.6
  361.4 81.8 reduce-scatter.4
